TPU v7x, 32 devices: a whole 2x2x4 slice. The times are simulated.
32 devices in a mesh: rep: 8 (over y, x, core), shard: 4 (over z).
Axes of the slice: x: 2, y: 2, z: 4, core: 2. Of those that a mesh axis runs over, the one named last changes fastest.
Arguments:
- inputs: bfloat16 [8, 4, 1104, 1024], P('rep', 'shard'), may hold values from -6 to 6
- counts: int32 [8], P('rep'), may hold values from 1 to 4, as said below
- ln1_gain: bfloat16 [1024], P('shard'), may hold values from 0.5 to 1.5
- ln1_shift: bfloat16 [1024], P('shard'), may hold values from -4 to 4
- w_qkv: bfloat16 [1024, 3072], P('shard'), may hold values from -0.1875 to 0.1875
- qv_bias: bfloat16 [2048], P('shard'), may hold values from -4 to 4
- w_out: bfloat16 [1024, 1024], P('shard'), may hold values from -0.75 to 0.75
- out_bias: bfloat16 [1024], P('shard'), may hold values from -4 to 4
- ln2_gain: bfloat16 [1024], P('shard'), may hold values from 0.5 to 1.5
- ln2_shift: bfloat16 [1024], P('shard'), may hold values from -4 to 4
- w_up: bfloat16 [1024, 4096], P('shard'), may hold values from -0.1875 to 0.1875
- up_bias: bfloat16 [4096], P('shard'), may hold values from -4 to 4
- w_down: bfloat16 [4096, 1024], P('shard'), may hold values from -0.09375 to 0.09375
- down_bias: bfloat16 [1024], P('shard'), may hold values from -4 to 4
- cotangent: bfloat16 [8, 4, 1104, 1024], P('rep', 'shard'), may hold values from -6 to 6
Outputs:
- output: bfloat16 [8, 4, 1104, 1024], P('rep', 'shard')
- input_grad: float32 [8, 4, 1104, 1024], P('rep', 'shard')
- grad_ln1_gain: float32 [1024], P('shard')
- grad_ln1_shift: float32 [1024], P('shard')
- grad_w_qkv: float32 [1024, 3072], P('shard')
- grad_qv_bias: float32 [2048], P('shard')
- grad_w_out: float32 [1024, 1024], P('shard')
- grad_out_bias: float32 [1024], P('shard')
- grad_ln2_gain: float32 [1024], P('shard')
- grad_ln2_shift: float32 [1024], P('shard')
- grad_w_up: float32 [1024, 4096], P('shard')
- grad_up_bias: float32 [4096], P('shard')
- grad_w_down: float32 [4096, 1024], P('shard')
- grad_down_bias: float32 [1024], P('shard')
Inputs may be any that keep to these rules, and one draw needn't show every extreme that they name: A group's live sequences occupy its slots 0 to counts - 1; some group has exactly 4 and some exactly 1.
All inputs are finite; a program needn't handle non-finite values.
Results may differ from a plain program's by a relative error of at most 0.018.
Values may be sent and summed in bfloat16 or wider, within the bound.
No kernel may reach another device: no remote copies, remote signals or barrier semaphores. Data moves between devices by JAX's collectives and lax.ppermute only.
A program may use at most 256 MiB of HBM per device.

v0:
```python
import jax
import jax.numpy as jnp
from jax import lax
from jax.sharding import PartitionSpec as P

HEADS = 16
HDIM = 64
eps = 1e-06
head_block = 4


def layer_norm(values, gain, shift):
    centre = values - jnp.mean(values, -1, keepdims=True)
    spread = jnp.mean(centre * centre, -1, keepdims=True)
    return centre * lax.rsqrt(spread + eps) * gain + shift


def gelu_exact(values):
    return jax.nn.gelu(values, approximate=False)


def matmul(left, right):
    return jnp.dot(left, right, preferred_element_type=jnp.float32)


def left_trans(left, right):
    return lax.dot_general(
        left, right, (((0,), (0,)), ((), ())), preferred_element_type=jnp.float32
    )


def right_trans(left, right):
    return lax.dot_general(
        left, right, (((1,), (1,)), ((), ())), preferred_element_type=jnp.float32
    )


def body(
    inputs,
    counts,
    ln1_gain,
    ln1_shift,
    w_qkv,
    qv_bias,
    w_out,
    out_bias,
    ln2_gain,
    ln2_shift,
    w_up,
    up_bias,
    w_down,
    down_bias,
    cotangent,
):
    gathered = (
        lax.all_gather(ln1_gain, "shard", axis=0, tiled=True),
        lax.all_gather(ln1_shift, "shard", axis=0, tiled=True),
        lax.all_gather(w_qkv, "shard", axis=0, tiled=True),
        lax.all_gather(qv_bias, "shard", axis=0, tiled=True),
        lax.all_gather(w_out, "shard", axis=0, tiled=True),
        lax.all_gather(out_bias, "shard", axis=0, tiled=True),
        lax.all_gather(ln2_gain, "shard", axis=0, tiled=True),
        lax.all_gather(ln2_shift, "shard", axis=0, tiled=True),
        lax.all_gather(w_up, "shard", axis=0, tiled=True),
        lax.all_gather(up_bias, "shard", axis=0, tiled=True),
        lax.all_gather(w_down, "shard", axis=0, tiled=True),
        lax.all_gather(down_bias, "shard", axis=0, tiled=True),
    )
    (
        full_g1,
        full_s1,
        full_qkv,
        full_qvb,
        full_wout,
        full_bout,
        full_g2,
        full_s2,
        full_wup,
        full_bup,
        full_wdown,
        full_bdown,
    ) = gathered
    slots = inputs.shape[1]
    seq_len = inputs.shape[2]
    width = inputs.shape[3]
    n_rows = slots * seq_len
    groups = HEADS // head_block
    scale = HDIM ** (-0.5)
    first_slot = lax.axis_index("shard") * slots
    alive = (jnp.arange(slots, dtype=jnp.int32) + first_slot < counts[0]).astype(jnp.float32)
    alive_rows = jnp.broadcast_to(alive[:, None], (slots, seq_len)).reshape(n_rows, 1)
    tokens = inputs.reshape(n_rows, width).astype(jnp.float32)
    hidden_one, norm_one_back = jax.vjp(
        layer_norm, tokens, full_g1.astype(jnp.float32), full_s1.astype(jnp.float32)
    )
    hidden_one_b = hidden_one.astype(jnp.bfloat16)
    projected = matmul(hidden_one_b, full_qkv)
    bias_f = full_qvb.astype(jnp.float32)
    queries_b = (projected[:, :width] + bias_f[:width]).astype(jnp.bfloat16)
    keys_b = projected[:, width : 2 * width].astype(jnp.bfloat16)
    values_b = (projected[:, 2 * width :] + bias_f[width:]).astype(jnp.bfloat16)

    def arrange(values):
        return values.reshape(slots, seq_len, groups, head_block, HDIM).transpose(2, 0, 1, 3, 4)

    def restore(values):
        return values.transpose(1, 2, 0, 3, 4).reshape(n_rows, width)

    query_groups = arrange(queries_b)
    key_groups = arrange(keys_b)
    value_groups = arrange(values_b)

    def forward_group(operands):
        query_part, key_part, value_part = operands
        scores = (
            jnp.einsum("cqhd,ckhd->chqk", query_part, key_part, preferred_element_type=jnp.float32)
            * scale
        )
        largest = jnp.max(scores, -1, keepdims=True)
        exponent = jnp.exp(scores - largest)
        denominator = jnp.sum(exponent, -1, keepdims=True)
        probs_b = (exponent / denominator).astype(jnp.bfloat16)
        mixed = jnp.einsum(
            "chqk,ckhd->cqhd", probs_b, value_part, preferred_element_type=jnp.float32
        )
        return (mixed, (largest + jnp.log(denominator))[..., 0])

    mixed_groups, log_totals = lax.map(forward_group, (query_groups, key_groups, value_groups))
    attended_b = restore(mixed_groups).astype(jnp.bfloat16)
    middle = tokens + matmul(attended_b, full_wout) + full_bout.astype(jnp.float32)
    hidden_two, norm_two_back = jax.vjp(
        layer_norm, middle, full_g2.astype(jnp.float32), full_s2.astype(jnp.float32)
    )
    hidden_two_b = hidden_two.astype(jnp.bfloat16)
    pre_act = matmul(hidden_two_b, full_wup) + full_bup.astype(jnp.float32)
    activated, gelu_back = jax.vjp(gelu_exact, pre_act)
    activated_b = activated.astype(jnp.bfloat16)
    result = middle + matmul(activated_b, full_wdown) + full_bdown.astype(jnp.float32)
    output = (alive_rows * result).astype(jnp.bfloat16).reshape(inputs.shape)
    again = (
        lax.all_gather(ln1_gain, "shard", axis=0, tiled=True),
        lax.all_gather(ln1_shift, "shard", axis=0, tiled=True),
        lax.all_gather(w_qkv, "shard", axis=0, tiled=True),
        lax.all_gather(qv_bias, "shard", axis=0, tiled=True),
        lax.all_gather(w_out, "shard", axis=0, tiled=True),
        lax.all_gather(out_bias, "shard", axis=0, tiled=True),
        lax.all_gather(ln2_gain, "shard", axis=0, tiled=True),
        lax.all_gather(ln2_shift, "shard", axis=0, tiled=True),
        lax.all_gather(w_up, "shard", axis=0, tiled=True),
        lax.all_gather(up_bias, "shard", axis=0, tiled=True),
        lax.all_gather(w_down, "shard", axis=0, tiled=True),
        lax.all_gather(down_bias, "shard", axis=0, tiled=True),
    )
    back_qkv = again[2]
    back_wout = again[4]
    back_wup = again[8]
    back_wdown = again[10]
    d_out = alive_rows * cotangent.reshape(n_rows, width).astype(jnp.float32)
    d_out_b = d_out.astype(jnp.bfloat16)
    grad_wdown = left_trans(activated_b, d_out_b)
    grad_bdown = jnp.sum(d_out, 0)
    d_act = right_trans(d_out_b, back_wdown)
    d_pre_b = gelu_back(d_act)[0].astype(jnp.bfloat16)
    grad_wup = left_trans(hidden_two_b, d_pre_b)
    grad_bup = jnp.sum(d_pre_b.astype(jnp.float32), 0)
    d_hidden_two = right_trans(d_pre_b, back_wup)
    d_mid_norm, grad_g2, grad_s2 = norm_two_back(d_hidden_two)
    d_mid = d_out + d_mid_norm
    d_proj_b = d_mid.astype(jnp.bfloat16)
    grad_wout = left_trans(attended_b, d_proj_b)
    grad_bout = jnp.sum(d_proj_b.astype(jnp.float32), 0)
    d_att_b = right_trans(d_proj_b, back_wout).astype(jnp.bfloat16)
    d_att_groups = arrange(d_att_b)

    def backward_group(operands):
        query_part, key_part, value_part, log_total, grad_part = operands
        scores = (
            jnp.einsum("cqhd,ckhd->chqk", query_part, key_part, preferred_element_type=jnp.float32)
            * scale
        )
        attn_probs = jnp.exp(scores - log_total[..., None])
        probs_b = attn_probs.astype(jnp.bfloat16)
        d_probs = jnp.einsum(
            "cqhd,ckhd->chqk", grad_part, value_part, preferred_element_type=jnp.float32
        )
        row_inner = jnp.sum(d_probs * attn_probs, -1, keepdims=True)
        d_scores_b = (attn_probs * (d_probs - row_inner)).astype(jnp.bfloat16)
        d_query = (
            jnp.einsum("chqk,ckhd->cqhd", d_scores_b, key_part, preferred_element_type=jnp.float32)
            * scale
        )
        d_key = (
            jnp.einsum(
                "chqk,cqhd->ckhd", d_scores_b, query_part, preferred_element_type=jnp.float32
            )
            * scale
        )
        d_value = jnp.einsum(
            "chqk,cqhd->ckhd", probs_b, grad_part, preferred_element_type=jnp.float32
        )
        return (d_query, d_key, d_value)

    d_query_groups, d_key_groups, d_value_groups = lax.map(
        backward_group, (query_groups, key_groups, value_groups, log_totals, d_att_groups)
    )
    d_qkv_b = jnp.concatenate(
        [restore(d_query_groups), restore(d_key_groups), restore(d_value_groups)], 1
    ).astype(jnp.bfloat16)
    grad_qkv = left_trans(hidden_one_b, d_qkv_b)
    column_sums = jnp.sum(d_qkv_b.astype(jnp.float32), 0)
    grad_qvb = jnp.concatenate([column_sums[:width], column_sums[2 * width :]])
    d_hidden_one = right_trans(d_qkv_b, back_qkv)
    d_in_norm, grad_g1, grad_s1 = norm_one_back(d_hidden_one)
    input_grad = (d_mid + d_in_norm).reshape(inputs.shape)
    owned = (
        lax.psum_scatter(
            grad_g1.astype(jnp.bfloat16), "shard", scatter_dimension=0, tiled=True
        ).astype(jnp.float32),
        lax.psum_scatter(
            grad_s1.astype(jnp.bfloat16), "shard", scatter_dimension=0, tiled=True
        ).astype(jnp.float32),
        lax.psum_scatter(
            grad_qkv.astype(jnp.bfloat16), "shard", scatter_dimension=0, tiled=True
        ).astype(jnp.float32),
        lax.psum_scatter(
            grad_qvb.astype(jnp.bfloat16), "shard", scatter_dimension=0, tiled=True
        ).astype(jnp.float32),
        lax.psum_scatter(
            grad_wout.astype(jnp.bfloat16), "shard", scatter_dimension=0, tiled=True
        ).astype(jnp.float32),
        lax.psum_scatter(
            grad_bout.astype(jnp.bfloat16), "shard", scatter_dimension=0, tiled=True
        ).astype(jnp.float32),
        lax.psum_scatter(
            grad_g2.astype(jnp.bfloat16), "shard", scatter_dimension=0, tiled=True
        ).astype(jnp.float32),
        lax.psum_scatter(
            grad_s2.astype(jnp.bfloat16), "shard", scatter_dimension=0, tiled=True
        ).astype(jnp.float32),
        lax.psum_scatter(
            grad_wup.astype(jnp.bfloat16), "shard", scatter_dimension=0, tiled=True
        ).astype(jnp.float32),
        lax.psum_scatter(
            grad_bup.astype(jnp.bfloat16), "shard", scatter_dimension=0, tiled=True
        ).astype(jnp.float32),
        lax.psum_scatter(
            grad_wdown.astype(jnp.bfloat16), "shard", scatter_dimension=0, tiled=True
        ).astype(jnp.float32),
        lax.psum_scatter(
            grad_bdown.astype(jnp.bfloat16), "shard", scatter_dimension=0, tiled=True
        ).astype(jnp.float32),
    )
    o_g1, o_s1, o_qkv, o_qvb, o_wout, o_bout, o_g2, o_s2, o_wup, o_bup, o_wdown, o_bdown = owned
    summed = (
        lax.psum(o_g1.astype(jnp.bfloat16), "rep").astype(jnp.float32),
        lax.psum(o_s1.astype(jnp.bfloat16), "rep").astype(jnp.float32),
        lax.psum(o_qkv.astype(jnp.bfloat16), "rep").astype(jnp.float32),
        lax.psum(o_qvb.astype(jnp.bfloat16), "rep").astype(jnp.float32),
        lax.psum(o_wout.astype(jnp.bfloat16), "rep").astype(jnp.float32),
        lax.psum(o_bout.astype(jnp.bfloat16), "rep").astype(jnp.float32),
        lax.psum(o_g2.astype(jnp.bfloat16), "rep").astype(jnp.float32),
        lax.psum(o_s2.astype(jnp.bfloat16), "rep").astype(jnp.float32),
        lax.psum(o_wup.astype(jnp.bfloat16), "rep").astype(jnp.float32),
        lax.psum(o_bup.astype(jnp.bfloat16), "rep").astype(jnp.float32),
        lax.psum(o_wdown.astype(jnp.bfloat16), "rep").astype(jnp.float32),
        lax.psum(o_bdown.astype(jnp.bfloat16), "rep").astype(jnp.float32),
    )
    return (
        output,
        input_grad,
        summed[0],
        summed[1],
        summed[2],
        summed[3],
        summed[4],
        summed[5],
        summed[6],
        summed[7],
        summed[8],
        summed[9],
        summed[10],
        summed[11],
    )


def solution(mesh):
    placed = (
        P("rep", "shard", None, None),
        P("rep"),
        P("shard"),
        P("shard"),
        P("shard", None),
        P("shard"),
        P("shard", None),
        P("shard"),
        P("shard"),
        P("shard"),
        P("shard", None),
        P("shard"),
        P("shard", None),
        P("shard"),
        P("rep", "shard", None, None),
    )
    return jax.shard_map(
        body,
        mesh=mesh,
        in_specs=placed,
        out_specs=(
            P("rep", "shard", None, None),
            P("rep", "shard", None, None),
            P("shard"),
            P("shard"),
            P("shard", None),
            P("shard"),
            P("shard", None),
            P("shard"),
            P("shard"),
            P("shard"),
            P("shard", None),
            P("shard"),
            P("shard", None),
            P("shard"),
        ),
        check_vma=False,
    )
```

profile of v0, /device:TPU:0, one launch (start us, length us, event | category | flops | bytes accessed | tf_op | source)
XLA Modules:
  0.0 1330.5 jit_solution(4466956774392505986)
XLA Ops:
  53.3 14.0 %all-gather = bf16[4,1,256]{2,1,0:T(2,128)(2,1)S(1)} all-gather(bf16[1,1,256]{2,1,0:T(2,128)(2,1)S(1)} %reshape.260), channel_id=1, replica_groups=mesh['rep'=8,'shard'=4] {'shard'}, dimensions={0}, use_global_device_ids=true | all-gather | bytes 2560 | tf_op jit(solution)/shard_map/all_gather | solution.py:56
  79.4 16.0 %all_gather.49 = bf16[4096]{0:T(1024)(128)(2,1)S(1)} all-gather(bf16[1024]{0:T(1024)(128)(2,1)S(1)} %copy-done.47), channel_id=1, replica_groups=mesh['rep'=8,'shard'=4] {'shard'}, dimensions={0}, use_global_device_ids=true | all-gather | bytes 10240 | tf_op jit(solution)/shard_map/all_gather | solution.py:65
  97.8 30.4 %all-gather.12.cloned.1.call-done = bf16[1024,3072]{1,0:T(8,128)(2,1)} async-done(((bf16[256,3072]{1,0:T(8,128)(2,1)}), bf16[1024,3072]{1,0:T(8,128)(2,1)}) %all-gather.12.cloned.1.call-update) | async-done | bytes 6291472 | tf_op jit(solution)/shard_map/all_gather | solution.py:58
  156.2 131.5 %while.26 = (s32[]{:T(128)}, bf16[4,1,1104,4,64]{2,4,3,1,0:T(8,128)(2,1)}, f32[4,1,4,1104]{3,2,1,0:T(4,128)}, bf16[4,1,1104,4,64]{2,4,3,1,0:T(8,128)(2,1)}, bf16...) while((s32[]{:T(128)}, bf16[4,1,1104,4,64]{2,4,3,1,0:T(8,128)(2,1)}, ...), condition=%wide.region_5.6_spmd, body=%wide.region_2.5_spmd.sunk | while | flops 1282190080 | bytes 62444376 | solution.py:128
  297.9 26.0 %all-gather.16.cloned.1.call-done = bf16[1024,4096]{1,0:T(8,128)(2,1)} async-done(((bf16[256,4096]{1,0:T(8,128)(2,1)}), bf16[1024,4096]{1,0:T(8,128)(2,1)}) %all-gather.16.cloned.1.call-update) | async-done | bytes 8388624 | tf_op jit(solution)/shard_map/all_gather | solution.py:64
  323.9 54.4 %multiply_convert_fusion.1 = (bf16[1104,4096]{1,0:T(8,128)(2,1)}, f32[1104,4096]{1,0:T(8,128)}, f32[1104,4096]{1,0:T(8,128)}) fusion(f32[4096]{0:T(1024)S(1)} %copy-done.39, bf16[1024,4096]{1,0:T(8,128)(2,1)} %all-gather.16.cloned.1.call-done, f32[1104,1024]{1,0:T(8,128)} %copy-done.8, f32[1024]{0:T(1024)S(1)} %bitcast.254, f32[1024]{0:T(1024)S(1)} %bitcast.248, ...), kind=kOutput, calls=%fused_computation.56 | convolution fusion | flops 9565126656 | bytes 58163840 | tf_op jit(solution)/shard_map/dot_general | solution.py:23
  378.3 94.9 %all-gather.18.cloned.1.call-done = bf16[4096,1024]{1,0:T(8,128)(2,1)} async-done(((bf16[1024,1024]{1,0:T(8,128)(2,1)}), bf16[4096,1024]{1,0:T(8,128)(2,1)}) %all-gather.18.cloned.1.call-update) | async-done | bytes 8388624 | tf_op jit(solution)/shard_map/all_gather | solution.py:66
  473.2 25.4 %fusion.92 = (bf16[4096]{0:T(1024)(128)(2,1)}, bf16[1104,4096]{1,0:T(8,128)(2,1)}) fusion(f32[1104,4096]{1,0:T(8,128)} %get-tuple-element.193, f32[1104,4096]{1,0:T(8,128)} %get-tuple-element.206, bf16[4096,1024]{1,0:T(8,128)(2,1)} %all-gather.18.cloned.1.call-done, bf16[1,1,1104,1024]{3,2,1,0:T(8,128)(2,1)S(1)} %copy-done.6, f32[]{:T(128)} %bitcast.22), kind=kOutput, calls=%fused_computation.137 | convolution fusion | flops 9332240384 | bytes 55877636 | tf_op jit(solution)/shard_map/dot_general | solution.py:33
  498.6 18.1 %multiply_reduce_fusion.1 = (bf16[1024]{0:T(1024)(128)(2,1)}, f32[1104]{0:T(1024)S(1)}, bf16[1024]{0:T(1024)(128)(2,1)}, f32[1104,1024]{1,0:T(8,128)S(1)}) fusion(f32[1104,1024]{1,0:T(8,128)} %copy-done.8, f32[1104]{0:T(1024)S(1)} %fusion.76, f32[1104]{0:T(1024)S(1)} %broadcast_multiply_fusion, f32[1024]{0:T(1024)S(1)} %bitcast.249, ...), kind=kOutput, calls=%fused_computation.102 | convolution fusion | flops 9270064128 | bytes 26497984 | tf_op jit(solution)/shard_map/dot_general | solution.py:33
  538.8 243.8 %while.27 = (s32[]{:T(128)}, bf16[4,1,1104,4,64]{2,4,3,1,0:T(8,128)(2,1)}, bf16[4,1,1104,4,64]{2,4,3,1,0:T(8,128)(2,1)}, bf16[4,1,1104,4,64]{2,4,3,1,0:T(8,128)(...) while((s32[]{:T(128)}, ...), condition=%wide.region_12.13_spmd, body=%wide.region_10.12_spmd.sunk | while | flops 3159731968 | bytes 219023680 | solution.py:203
  560.7 17.6 %multiply_reduce_fusion.5 = (f32[4,1104]{1,0:T(4,128)S(1)}, f32[4,1104,1104]{1,2,0:T(8,128)}) fusion(f32[4,1104,1104]{1,2,0:T(8,128)} %fusion.140, bf16[4,1,1104,4,64]{2,4,3,1,0:T(8,128)(2,1)} %get-tuple-element.360, s32[]{:T(128)S(6)} %copy.89, bf16[4,1,1104,4,64]{2,4,3,1,0:T(8,128)(2,1)S(1)} %copy-done.5), kind=kOutput, calls=%fused_computation.20.clone.1 | convolution fusion | flops 633779904 | bytes 41048320 | tf_op jit(solution)/shard_map/while/body/eval_jaxpr/cqhd,ckhd->chqk/dot_general | solution.py:183
  578.4 13.5 %multiply_convert_fusion.3 = bf16[4,1104,1104]{1,2,0:T(8,128)(2,1)S(1)} fusion(f32[4,1104,1104]{1,2,0:T(8,128)} %fusion.140, f32[4,1104,1104]{1,2,0:T(8,128)} %get-tuple-element.309, f32[4,1104]{1,0:T(4,128)S(1)} %get-tuple-element.310), kind=kLoop, calls=%fused_computation.19.clone.1 | loop fusion | flops 14625792 | bytes 48770304 | tf_op jit(solution)/shard_map/while/body/eval_jaxpr/convert_element_type | solution.py:187
  621.6 17.5 %multiply_reduce_fusion.5 = (f32[4,1104]{1,0:T(4,128)S(1)}, f32[4,1104,1104]{1,2,0:T(8,128)}) fusion(f32[4,1104,1104]{1,2,0:T(8,128)} %fusion.140, bf16[4,1,1104,4,64]{2,4,3,1,0:T(8,128)(2,1)} %get-tuple-element.360, s32[]{:T(128)S(6)} %copy.89, bf16[4,1,1104,4,64]{2,4,3,1,0:T(8,128)(2,1)S(1)} %copy-done.5), kind=kOutput, calls=%fused_computation.20.clone.1 | convolution fusion | flops 633779904 | bytes 41048320 | tf_op jit(solution)/shard_map/while/body/eval_jaxpr/cqhd,ckhd->chqk/dot_general | solution.py:183
  639.2 13.5 %multiply_convert_fusion.3 = bf16[4,1104,1104]{1,2,0:T(8,128)(2,1)S(1)} fusion(f32[4,1104,1104]{1,2,0:T(8,128)} %fusion.140, f32[4,1104,1104]{1,2,0:T(8,128)} %get-tuple-element.309, f32[4,1104]{1,0:T(4,128)S(1)} %get-tuple-element.310), kind=kLoop, calls=%fused_computation.19.clone.1 | loop fusion | flops 14625792 | bytes 48770304 | tf_op jit(solution)/shard_map/while/body/eval_jaxpr/convert_element_type | solution.py:187
  682.5 17.5 %multiply_reduce_fusion.5 = (f32[4,1104]{1,0:T(4,128)S(1)}, f32[4,1104,1104]{1,2,0:T(8,128)}) fusion(f32[4,1104,1104]{1,2,0:T(8,128)} %fusion.140, bf16[4,1,1104,4,64]{2,4,3,1,0:T(8,128)(2,1)} %get-tuple-element.360, s32[]{:T(128)S(6)} %copy.89, bf16[4,1,1104,4,64]{2,4,3,1,0:T(8,128)(2,1)S(1)} %copy-done.5), kind=kOutput, calls=%fused_computation.20.clone.1 | convolution fusion | flops 633779904 | bytes 41048320 | tf_op jit(solution)/shard_map/while/body/eval_jaxpr/cqhd,ckhd->chqk/dot_general | solution.py:183
  743.3 17.5 %multiply_reduce_fusion.5 = (f32[4,1104]{1,0:T(4,128)S(1)}, f32[4,1104,1104]{1,2,0:T(8,128)}) fusion(f32[4,1104,1104]{1,2,0:T(8,128)} %fusion.140, bf16[4,1,1104,4,64]{2,4,3,1,0:T(8,128)(2,1)} %get-tuple-element.360, s32[]{:T(128)S(6)} %copy.89, bf16[4,1,1104,4,64]{2,4,3,1,0:T(8,128)(2,1)S(1)} %copy-done.5), kind=kOutput, calls=%fused_computation.20.clone.1 | convolution fusion | flops 633779904 | bytes 41048320 | tf_op jit(solution)/shard_map/while/body/eval_jaxpr/cqhd,ckhd->chqk/dot_general | solution.py:183
  782.6 15.3 %convolution_convert_fusion.2 = bf16[1024,3072]{1,0:T(8,128)(2,1)} fusion(bf16[1,1,1104,1024]{3,2,1,0:T(8,128)(2,1)} %param.19, f32[1024]{0:T(1024)S(1)} %bitcast.257, f32[1024]{0:T(1024)S(1)} %bitcast.244, f32[1104]{0:T(1024)S(1)} %copy-done.24, f32[1104]{0:T(1024)S(1)} %copy-done.22, bf16[1104,1024]{0,1:T(8,128)(2,1)} %bitcast.232, ...), kind=kOutput, calls=%fused_computation.75 | convolution fusion | flops 6976045056 | bytes 15352448 | tf_op jit(solution)/shard_map/dot_general | solution.py:27
  798.6 18.7 %convolution_convert_fusion.1 = bf16[1024,4096]{1,0:T(8,128)(2,1)} fusion(bf16[1104,4096]{1,0:T(8,128)(2,1)} %get-tuple-element.210, f32[1104,1024]{1,0:T(8,128)} %copy-done.8, f32[1024]{0:T(1024)S(1)} %bitcast.255, f32[1024]{0:T(1024)S(1)} %bitcast.251, f32[1104]{0:T(1024)S(1)} %copy-done.36, f32[1104]{0:T(1024)S(1)} %copy-done.26), kind=kOutput, calls=%fused_computation.71 | convolution fusion | flops 9270870016 | bytes 21971584 | tf_op jit(solution)/shard_map/dot_general | solution.py:27
  818.9 17.4 %convolution_convert_fusion = bf16[4096,1024]{1,0:T(8,128)(2,1)} fusion(bf16[1104,4096]{1,0:T(8,128)(2,1)} %get-tuple-element.192, bf16[1,1,1104,1024]{3,2,1,0:T(8,128)(2,1)S(1)} %copy-done.7, f32[]{:T(128)} %bitcast.22), kind=kOutput, calls=%fused_computation.70 | convolution fusion | flops 9268609024 | bytes 19693572 | tf_op jit(solution)/shard_map/dot_general | solution.py:27
  872.0 22.2 %all-reduce.10 = (bf16[1024]{0:T(1024)(128)(2,1)S(1)}, bf16[1024]{0:T(1024)(128)(2,1)S(1)}, bf16[2048]{0:T(1024)(128)(2,1)S(1)}, bf16[1024]{0:T(1024)(128)(2,1)S...) all-reduce(bf16[1024]{0:T(1024)(128)(2,1)S(1)} %get-tuple-element.1, ...), channel_id=2, replica_groups=mesh['rep'=8,'shard'=4] {'shard'}, use_global_device_ids=true, to_apply=%region_16.17.clone | all-reduce | flops 12288 | bytes 49152
  911.8 143.8 %reduce-scatter.9.cloned.1.call-done = bf16[256,4096]{1,0:T(8,128)(2,1)} async-done(((bf16[1024,4096]{1,0:T(8,128)(2,1)}), bf16[256,4096]{1,0:T(8,128)(2,1)}) %reduce-scatter.9.cloned.1.call-update) | async-done | bytes 2097168 | tf_op jit(solution)/shard_map/reduce_scatter | solution.py:240
  1055.6 147.7 %reduce-scatter.11.cloned.1.call-done = bf16[1024,1024]{1,0:T(8,128)(2,1)} async-done(((bf16[4096,1024]{1,0:T(8,128)(2,1)}), bf16[1024,1024]{1,0:T(8,128)(2,1)}) %reduce-scatter.11.cloned.1.call-update) | async-done | bytes 2097168 | tf_op jit(solution)/shard_map/reduce_scatter | solution.py:246
  1210.1 17.3 %fusion.72 = bf16[1,1,1104,1024]{3,2,1,0:T(8,128)(2,1)} fusion(f32[1104,1024]{1,0:T(8,128)} %copy-done.8, bf16[1104,4096]{1,0:T(8,128)(2,1)} %get-tuple-element.192, bf16[4096,1024]{1,0:T(8,128)(2,1)} %all-gather.18.cloned.1.call-done, f32[1024]{0:T(1024)S(1)} %bitcast.258, f32[]{:T(128)} %bitcast.22), kind=kOutput, calls=%fused_computation.111 | convolution fusion | flops 9265545216 | bytes 24219652 | tf_op jit(solution)/shard_map/dot_general | solution.py:23
  1227.4 85.5 %all-reduce.13.cloned.1.call-done = (bf16[256,3072]{1,0:T(8,128)(2,1)}, bf16[256,1024]{1,0:T(8,128)(2,1)}, bf16[256,4096]{1,0:T(8,128)(2,1)}, bf16[1024,1024]{1,0:T(8,128)(2,1)}) async-done(((bf16[256,3072]{1,0:T(8,128)(2,1)}, bf16[256,1024]{1,0:T(8,128)(2,1)}, bf16[256,4096]{1,0:T(8,128)(2,1)}, bf16[1024,1024]{1,0:T(8,128)(2,1)}), (bf16[256,3072]{1,0:T(8,128)(2,1)}, bf16[256,1024]{1,0:T(8,128)(2,1)}, ...) | async-done | bytes 6291472 | tf_op jit(solution)/shard_map/psum | solution.py:257
  (295 shorter events, 467.9 us)
Async XLA Ops:
  7.2 72.2 %copy-start.47 = (bf16[1024]{0:T(1024)(128)(2,1)S(1)}, bf16[1024]{0:T(1024)(128)(2,1)}, u32[]{:S(2)}) copy-start(bf16[1024]{0:T(1024)(128)(2,1)} %param.30) | copy-start | bytes 6148
  7.3 88.8 %copy-start.3 = (bf16[1,1,1104,1024]{3,2,1,0:T(8,128)(2,1)S(1)}, bf16[1,1,1104,1024]{3,2,1,0:T(8,128)(2,1)}, u32[]{:S(2)}) copy-start(bf16[1,1,1104,1024]{3,2,1,0:T(8,128)(2,1)} %param.19) | copy-start | bytes 6782980
  7.3 120.9 %all-gather.12.cloned.1.call-start = ((), (), s32[]{:S(2)}) async-start(), calls=%async_computation.4 | async-start | bytes 7864320 | tf_op jit(solution)/shard_map/all_gather | solution.py:58
  8.0 279.7 %all-gather.14.cloned.1.call-start = ((), (), s32[]{:S(2)}) async-start(), calls=%async_computation.5 | async-start | bytes 2621440 | tf_op jit(solution)/shard_map/all_gather | solution.py:60
  8.7 315.1 %all-gather.16.cloned.1.call-start = ((), (), s32[]{:S(2)}) async-start(), calls=%async_computation.6 | async-start | bytes 10485760 | tf_op jit(solution)/shard_map/all_gather | solution.py:64
  9.5 463.7 %all-gather.18.cloned.1.call-start = ((), (), s32[]{:S(2)}) async-start(), calls=%async_computation.7 | async-start | bytes 10485760 | tf_op jit(solution)/shard_map/all_gather | solution.py:66
  10.1 901.8 %reduce-scatter.7.cloned.1.call-start = ((), (), s32[]{:S(2)}) async-start(), calls=%async_computation.9 | async-start | bytes 2621440 | tf_op jit(solution)/shard_map/reduce_scatter | solution.py:228
  53.3 84.6 %copy-start.44 = (f32[4,1,256]{2,1,0:T(1,128)}, f32[4,1,256]{2,1,0:T(1,128)S(1)}, u32[]{:S(2)}) copy-start(f32[4,1,256]{2,1,0:T(1,128)S(1)} %convert_element_type.230) | copy-start | bytes 12292
  67.3 70.5 %copy-start.33 = (f32[4,1,256]{2,1,0:T(1,128)}, f32[4,1,256]{2,1,0:T(1,128)S(1)}, u32[]{:S(2)}) copy-start(f32[4,1,256]{2,1,0:T(1,128)S(1)} %convert_element_type.229) | copy-start | bytes 12292
  96.4 41.4 %copy-start.21 = (f32[1104]{0:T(1024)}, f32[1104]{0:T(1024)S(1)}, u32[]{:S(2)}) copy-start(f32[1104]{0:T(1024)S(1)} %broadcast_multiply_fusion.1) | copy-start | bytes 13252
  97.8 40.1 %copy-start.23 = (f32[1104]{0:T(1024)}, f32[1104]{0:T(1024)S(1)}, u32[]{:S(2)}) copy-start(f32[1104]{0:T(1024)S(1)} %fusion.75) | copy-start | bytes 13252
  156.2 131.5 %copy-start.46 = (f32[4,1,256]{2,1,0:T(1,128)S(1)}, f32[4,1,256]{2,1,0:T(1,128)}, u32[]{:S(2)}) copy-start(f32[4,1,256]{2,1,0:T(1,128)} %convert_element_type.232) | copy-start | bytes 12292
  294.6 222.1 %copy-start.25 = (f32[1104]{0:T(1024)}, f32[1104]{0:T(1024)S(1)}, u32[]{:S(2)}) copy-start(f32[1104]{0:T(1024)S(1)} %broadcast_multiply_fusion) | copy-start | bytes 13252
  297.9 218.8 %copy-start.35 = (f32[1104]{0:T(1024)}, f32[1104]{0:T(1024)S(1)}, u32[]{:S(2)}) copy-start(f32[1104]{0:T(1024)S(1)} %fusion.76) | copy-start | bytes 13252
  323.9 149.3 %copy-start.6 = (bf16[1,1,1104,1024]{3,2,1,0:T(8,128)(2,1)S(1)}, bf16[1,1,1104,1024]{3,2,1,0:T(8,128)(2,1)}, u32[]{:S(2)}) copy-start(bf16[1,1,1104,1024]{3,2,1,0:T(8,128)(2,1)} %param.33) | copy-start | bytes 6782980
  526.0 385.8 %reduce-scatter.5.cloned.1.call-start = ((), (), s32[]{:S(2)}) async-start(), calls=%async_computation.8 | async-start | bytes 7864320 | tf_op jit(solution)/shard_map/reduce_scatter | solution.py:222
  538.8 243.8 %copy-start.22 = (f32[1104]{0:T(1024)S(1)}, f32[1104]{0:T(1024)}, u32[]{:S(2)}) copy-start(f32[1104]{0:T(1024)} %copy-done.21) | copy-start | bytes 13252
  538.8 243.8 %copy-start.24 = (f32[1104]{0:T(1024)S(1)}, f32[1104]{0:T(1024)}, u32[]{:S(2)}) copy-start(f32[1104]{0:T(1024)} %copy-done.23) | copy-start | bytes 13252
  538.8 243.8 %copy-start.34 = (f32[4,1,256]{2,1,0:T(1,128)S(1)}, f32[4,1,256]{2,1,0:T(1,128)}, u32[]{:S(2)}) copy-start(f32[4,1,256]{2,1,0:T(1,128)} %copy-done.33) | copy-start | bytes 12292
  538.8 243.8 %copy-start.45 = (f32[4,1,256]{2,1,0:T(1,128)S(1)}, f32[4,1,256]{2,1,0:T(1,128)}, u32[]{:S(2)}) copy-start(f32[4,1,256]{2,1,0:T(1,128)} %copy-done.44) | copy-start | bytes 12292
  797.9 257.7 %reduce-scatter.9.cloned.1.call-start = ((), (), s32[]{:S(2)}) async-start(), calls=%async_computation.10 | async-start | bytes 10485760 | tf_op jit(solution)/shard_map/reduce_scatter | solution.py:240
  817.3 386.0 %reduce-scatter.11.cloned.1.call-start = ((), (), s32[]{:S(2)}) async-start(), calls=%async_computation.11 | async-start | bytes 10485760 | tf_op jit(solution)/shard_map/reduce_scatter | solution.py:246
  836.3 476.6 %all-reduce.13.cloned.1.call-start = ((), (), s32[]{:S(2)}) async-start(), calls=%async_computation.12 | async-start | bytes 12582912 | tf_op jit(solution)/shard_map/psum | solution.py:257
  872.0 331.4 %copy-start.32 = (f32[1104]{0:T(1024)S(1)}, f32[1104]{0:T(1024)}, u32[]{:S(2)}) copy-start(f32[1104]{0:T(1024)} %copy-done.31) | copy-start | bytes 13252
  (64 other events, 476.7 us)
Sparse Core Ops, SparseCore 0:
  9.7 118.4 all-gather.11
  129.7 44.1 all-gather.13
  175.5 148.3 all-gather.15
  325.3 147.8 all-gather.17
  526.1 42.0 reduce-scatter.6
  798.1 110.0 reduce-scatter.4
  910.7 144.9 reduce-scatter.8
  1058.1 145.1 reduce-scatter.10
  1207.4 105.4 all-reduce.12
where the time goes:
time: 1340 us; the launch traced here: 1330 us
  waiting for transfers between devices  531 us (40%)
  matrix products  475 us (35%)
  other arithmetic  137 us (10%)
  blocking collectives  125 us (9%)
  local copies, waits for them, and re-layouts  42.8 us (3%)
  between operations  17.3 us (1%)
    reduce_scatter x1, waiting for transfers between devices, body(): lax.psum_scatter(grad_wdown.astype(jnp.bfloat16), 'shard', scatter_dimens...  148 us
    reduce_scatter x1, waiting for transfers between devices, body(): lax.psum_scatter(grad_wup.astype(jnp.bfloat16), 'shard', scatter_dimensio...  144 us
    all_gather x1, waiting for transfers between devices, body(): lax.all_gather(w_down, 'shard', axis=0, tiled=True)  94.9 us
    dot_general x4, matrix products, matmul(): return jnp.dot(left, right, preferred_element_type=jnp.float32)  88.1 us
    psum x1, waiting for transfers between devices, body(): lax.psum(o_qkv.astype(jnp.bfloat16), 'rep').astype(jnp.float32)  85.5 us
    dot_general x4, matrix products, backward_group(): jnp.einsum('cqhd,ckhd->chqk', grad_part, value_part, preferred_element_ty...  70.2 us
    dot_general x4, matrix products, right_trans(): lax.dot_general(left, right, (((1,), (1,)), ((), ())), preferred_element_...  61 us
    dot_general x4, matrix products, left_trans(): lax.dot_general(left, right, (((0,), (0,)), ((), ())), preferred_element_...  55.5 us
  transfers between devices with their start and end apart: 9, of which 6 were waited for; matrix products, arithmetic and copies ran while one was open for 43% of the time, Pallas kernels for 0%

commit v1 on v0

--- a/solution.py
+++ b/solution.py
@@ -52,6 +52,11 @@
     down_bias,
     cotangent,
 ):
+
+    def create_row(vec):
+        low = lax.all_gather(vec, axis_name="rep").sum(axis=0)
+        return low
+
     gathered = (
         lax.all_gather(ln1_gain, "shard", axis=0, tiled=True),
         lax.all_gather(ln1_shift, "shard", axis=0, tiled=True),
@@ -254,7 +259,7 @@
     summed = (
         lax.psum(o_g1.astype(jnp.bfloat16), "rep").astype(jnp.float32),
         lax.psum(o_s1.astype(jnp.bfloat16), "rep").astype(jnp.float32),
-        lax.psum(o_qkv.astype(jnp.bfloat16), "rep").astype(jnp.float32),
+        create_row(o_qkv.astype(jnp.bfloat16)).astype(jnp.float32),
         lax.psum(o_qvb.astype(jnp.bfloat16), "rep").astype(jnp.float32),
         lax.psum(o_wout.astype(jnp.bfloat16), "rep").astype(jnp.float32),
         lax.psum(o_bout.astype(jnp.bfloat16), "rep").astype(jnp.float32),

time: 1340 us -> 1170 us (0.87)
  waiting for transfers between devices: 531 us -> 353 us
    reduce_scatter x1, waiting for transfers between devices: 144 us -> 0.02 us  [body(): lax.psum_scatter(grad_wup.astype(jnp.bfloat16), 'shard', scatter_dimensio...]
    reduce_scatter x1, waiting for transfers between devices: 148 us -> 23.1 us  [body(): lax.psum_scatter(grad_wdown.astype(jnp.bfloat16), 'shard', scatter_dimens...]
    reduce_scatter x1, waiting for transfers between devices: 0.01 us -> 114 us  [body(): lax.psum_scatter(grad_qkv.astype(jnp.bfloat16), 'shard', scatter_dimensio...]
    psum x1, waiting for transfers between devices: 85.5 us -> 0.01 us  [body(): lax.psum(o_wout.astype(jnp.bfloat16), 'rep').astype(jnp.float32)]
    all_gather x0 -> x1, waiting for transfers between devices: none -> 62.6 us  [create_row(): low = lax.all_gather(vec, axis_name='rep').sum(axis=0)]
  transfers between devices with their start and end apart: 9 -> 10, of which waited for: 6 -> 6; matrix products, arithmetic and copies ran while one was open for 43% -> 51% of each run, Pallas kernels for 0% -> 0%
where the time goes in v1:
time: 1170 us; the launch traced here: 1160 us
  matrix products  477 us (41%)
  waiting for transfers between devices  353 us (30%)
  other arithmetic  145 us (12%)
  blocking collectives  122 us (10%)
  local copies, waits for them, and re-layouts  41.7 us (4%)
  between operations  17.9 us (2%)
    reduce_scatter x1, waiting for transfers between devices, body(): lax.psum_scatter(grad_qkv.astype(jnp.bfloat16), 'shard', scatter_dimensio...  114 us
    all_gather x1, waiting for transfers between devices, body(): lax.all_gather(w_down, 'shard', axis=0, tiled=True)  94.8 us
    dot_general x4, matrix products, matmul(): return jnp.dot(left, right, preferred_element_type=jnp.float32)  87.4 us
    dot_general x4, matrix products, backward_group(): jnp.einsum('cqhd,ckhd->chqk', grad_part, value_part, preferred_element_ty...  71.2 us
    all_gather x1, waiting for transfers between devices, create_row(): low = lax.all_gather(vec, axis_name='rep').sum(axis=0)  62.6 us
    dot_general x4, matrix products, right_trans(): lax.dot_general(left, right, (((1,), (1,)), ((), ())), preferred_element_...  62.3 us
    dot_general x4, matrix products, left_trans(): lax.dot_general(left, right, (((0,), (0,)), ((), ())), preferred_element_...  55.1 us
    convert_element_type x4, other arithmetic, backward_group(): d_scores_b = (attn_probs * (d_probs - row_inner)).astype(jnp.bfloat16)  54.7 us
  transfers between devices with their start and end apart: 10, of which 6 were waited for; matrix products, arithmetic and copies ran while one was open for 51% of the time, Pallas kernels for 0%

profile of v1, /device:TPU:0, one launch (start us, length us, event | category | flops | bytes accessed | tf_op | source)
XLA Modules:
  0.0 1158.9 jit_solution(7479079227967921735)
XLA Ops:
  53.3 14.0 %all-gather.1 = bf16[4,1,256]{2,1,0:T(2,128)(2,1)S(1)} all-gather(bf16[1,1,256]{2,1,0:T(2,128)(2,1)S(1)} %reshape.261), channel_id=1, replica_groups=mesh['rep'=8,'shard'=4] {'shard'}, dimensions={0}, use_global_device_ids=true | all-gather | bytes 2560 | tf_op jit(solution)/shard_map/all_gather | solution.py:61
  79.4 16.0 %all_gather.55 = bf16[4096]{0:T(1024)(128)(2,1)S(1)} all-gather(bf16[1024]{0:T(1024)(128)(2,1)S(1)} %copy-done.39), channel_id=1, replica_groups=mesh['rep'=8,'shard'=4] {'shard'}, dimensions={0}, use_global_device_ids=true | all-gather | bytes 10240 | tf_op jit(solution)/shard_map/all_gather | solution.py:70
  97.8 30.4 %all-gather.14.cloned.1.call-done = bf16[1024,3072]{1,0:T(8,128)(2,1)} async-done(((bf16[256,3072]{1,0:T(8,128)(2,1)}), bf16[1024,3072]{1,0:T(8,128)(2,1)}) %all-gather.14.cloned.1.call-update) | async-done | bytes 6291472 | tf_op jit(solution)/shard_map/all_gather | solution.py:63
  156.2 131.8 %while.26 = (s32[]{:T(128)}, bf16[4,1,1104,4,64]{2,4,3,1,0:T(8,128)(2,1)}, f32[4,1,4,1104]{3,2,1,0:T(4,128)}, bf16[4,1,1104,4,64]{2,4,3,1,0:T(8,128)(2,1)}, bf16...) while((s32[]{:T(128)}, bf16[4,1,1104,4,64]{2,4,3,1,0:T(8,128)(2,1)}, ...), condition=%wide.region_5.6_spmd, body=%wide.region_2.5_spmd.sunk | while | flops 1282190080 | bytes 62444376 | solution.py:133
  298.2 25.7 %all-gather.18.cloned.1.call-done = bf16[1024,4096]{1,0:T(8,128)(2,1)} async-done(((bf16[256,4096]{1,0:T(8,128)(2,1)}), bf16[1024,4096]{1,0:T(8,128)(2,1)}) %all-gather.18.cloned.1.call-update) | async-done | bytes 8388624 | tf_op jit(solution)/shard_map/all_gather | solution.py:69
  323.9 54.5 %multiply_convert_fusion.1 = (bf16[1104,4096]{1,0:T(8,128)(2,1)}, f32[1104,4096]{1,0:T(8,128)}, f32[1104,4096]{1,0:T(8,128)}) fusion(f32[4096]{0:T(1024)S(1)} %copy-done.32, bf16[1024,4096]{1,0:T(8,128)(2,1)} %all-gather.18.cloned.1.call-done, f32[1104,1024]{1,0:T(8,128)} %copy-done.7, f32[1024]{0:T(1024)S(1)} %bitcast.258, f32[1024]{0:T(1024)S(1)} %bitcast.250, ...), kind=kOutput, calls=%fused_computation.56 | convolution fusion | flops 9565126656 | bytes 58163840 | tf_op jit(solution)/shard_map/dot_general | solution.py:23
  378.4 94.8 %all-gather.20.cloned.1.call-done = bf16[4096,1024]{1,0:T(8,128)(2,1)} async-done(((bf16[1024,1024]{1,0:T(8,128)(2,1)}), bf16[4096,1024]{1,0:T(8,128)(2,1)}) %all-gather.20.cloned.1.call-update) | async-done | bytes 8388624 | tf_op jit(solution)/shard_map/all_gather | solution.py:71
  473.2 25.1 %fusion.92 = (bf16[4096]{0:T(1024)(128)(2,1)}, bf16[1104,4096]{1,0:T(8,128)(2,1)}) fusion(f32[1104,4096]{1,0:T(8,128)} %get-tuple-element.192, f32[1104,4096]{1,0:T(8,128)} %get-tuple-element.205, bf16[4096,1024]{1,0:T(8,128)(2,1)} %all-gather.20.cloned.1.call-done, bf16[1,1,1104,1024]{3,2,1,0:T(8,128)(2,1)S(1)} %copy-done.6, f32[]{:T(128)} %bitcast.22), kind=kOutput, calls=%fused_computation.137 | convolution fusion | flops 9332240384 | bytes 55877636 | tf_op jit(solution)/shard_map/dot_general | solution.py:33
  498.3 18.1 %multiply_reduce_fusion.1 = (bf16[1024]{0:T(1024)(128)(2,1)}, f32[1104]{0:T(1024)S(1)}, bf16[1024]{0:T(1024)(128)(2,1)}, f32[1104,1024]{1,0:T(8,128)S(1)}) fusion(f32[1104,1024]{1,0:T(8,128)} %copy-done.7, f32[1104]{0:T(1024)S(1)} %fusion.76, f32[1104]{0:T(1024)S(1)} %broadcast_multiply_fusion, f32[1024]{0:T(1024)S(1)} %bitcast.251, ...), kind=kOutput, calls=%fused_computation.102 | convolution fusion | flops 9270064128 | bytes 26497984 | tf_op jit(solution)/shard_map/dot_general | solution.py:33
  526.0 17.9 %convolution_convert_fusion.1 = bf16[1024,4096]{1,0:T(8,128)(2,1)} fusion(bf16[1104,4096]{1,0:T(8,128)(2,1)} %get-tuple-element.209, f32[1104,1024]{1,0:T(8,128)} %copy-done.7, f32[1024]{0:T(1024)S(1)} %bitcast.259, f32[1024]{0:T(1024)S(1)} %bitcast.253, f32[1104]{0:T(1024)S(1)} %fusion.76, f32[1104]{0:T(1024)S(1)} %broadcast_multiply_fusion), kind=kOutput, calls=%fused_computation.71 | convolution fusion | flops 9270870016 | bytes 21971584 | tf_op jit(solution)/shard_map/dot_general | solution.py:27
  554.4 17.4 %convolution_convert_fusion = bf16[4096,1024]{1,0:T(8,128)(2,1)} fusion(bf16[1104,4096]{1,0:T(8,128)(2,1)} %get-tuple-element.191, bf16[1,1,1104,1024]{3,2,1,0:T(8,128)(2,1)S(1)} %copy-done.6, f32[]{:T(128)} %bitcast.22), kind=kOutput, calls=%fused_computation.70 | convolution fusion | flops 9268609024 | bytes 19693572 | tf_op jit(solution)/shard_map/dot_general | solution.py:27
  577.1 246.2 %while.27 = (s32[]{:T(128)}, bf16[4,1,1104,4,64]{2,4,3,1,0:T(8,128)(2,1)}, bf16[4,1,1104,4,64]{2,4,3,1,0:T(8,128)(2,1)}, bf16[4,1,1104,4,64]{2,4,3,1,0:T(8,128)(...) while((s32[]{:T(128)}, ...), condition=%wide.region_12.13_spmd, body=%wide.region_10.12_spmd.sunk | while | flops 3159731968 | bytes 219023680 | solution.py:208
  599.1 17.6 %multiply_reduce_fusion.5 = (f32[4,1104]{1,0:T(4,128)S(1)}, f32[4,1104,1104]{1,2,0:T(8,128)}) fusion(f32[4,1104,1104]{1,2,0:T(8,128)} %fusion.140, bf16[4,1,1104,4,64]{2,4,3,1,0:T(8,128)(2,1)} %get-tuple-element.359, s32[]{:T(128)S(6)} %copy.89, bf16[4,1,1104,4,64]{2,4,3,1,0:T(8,128)(2,1)S(1)} %copy-done.5), kind=kOutput, calls=%fused_computation.20.clone.1 | convolution fusion | flops 633779904 | bytes 41048320 | tf_op jit(solution)/shard_map/while/body/eval_jaxpr/cqhd,ckhd->chqk/dot_general | solution.py:188
  660.5 17.6 %multiply_reduce_fusion.5 = (f32[4,1104]{1,0:T(4,128)S(1)}, f32[4,1104,1104]{1,2,0:T(8,128)}) fusion(f32[4,1104,1104]{1,2,0:T(8,128)} %fusion.140, bf16[4,1,1104,4,64]{2,4,3,1,0:T(8,128)(2,1)} %get-tuple-element.359, s32[]{:T(128)S(6)} %copy.89, bf16[4,1,1104,4,64]{2,4,3,1,0:T(8,128)(2,1)S(1)} %copy-done.5), kind=kOutput, calls=%fused_computation.20.clone.1 | convolution fusion | flops 633779904 | bytes 41048320 | tf_op jit(solution)/shard_map/while/body/eval_jaxpr/cqhd,ckhd->chqk/dot_general | solution.py:188
  678.2 13.7 %multiply_convert_fusion.3 = bf16[4,1104,1104]{1,2,0:T(8,128)(2,1)S(1)} fusion(f32[4,1104,1104]{1,2,0:T(8,128)} %fusion.140, f32[4,1104,1104]{1,2,0:T(8,128)} %get-tuple-element.308, f32[4,1104]{1,0:T(4,128)S(1)} %get-tuple-element.309), kind=kLoop, calls=%fused_computation.19.clone.1 | loop fusion | flops 14625792 | bytes 48770304 | tf_op jit(solution)/shard_map/while/body/eval_jaxpr/convert_element_type | solution.py:192
  721.8 18.1 %multiply_reduce_fusion.5 = (f32[4,1104]{1,0:T(4,128)S(1)}, f32[4,1104,1104]{1,2,0:T(8,128)}) fusion(f32[4,1104,1104]{1,2,0:T(8,128)} %fusion.140, bf16[4,1,1104,4,64]{2,4,3,1,0:T(8,128)(2,1)} %get-tuple-element.359, s32[]{:T(128)S(6)} %copy.89, bf16[4,1,1104,4,64]{2,4,3,1,0:T(8,128)(2,1)S(1)} %copy-done.5), kind=kOutput, calls=%fused_computation.20.clone.1 | convolution fusion | flops 633779904 | bytes 41048320 | tf_op jit(solution)/shard_map/while/body/eval_jaxpr/cqhd,ckhd->chqk/dot_general | solution.py:188
  783.5 17.8 %multiply_reduce_fusion.5 = (f32[4,1104]{1,0:T(4,128)S(1)}, f32[4,1104,1104]{1,2,0:T(8,128)}) fusion(f32[4,1104,1104]{1,2,0:T(8,128)} %fusion.140, bf16[4,1,1104,4,64]{2,4,3,1,0:T(8,128)(2,1)} %get-tuple-element.359, s32[]{:T(128)S(6)} %copy.89, bf16[4,1,1104,4,64]{2,4,3,1,0:T(8,128)(2,1)S(1)} %copy-done.5), kind=kOutput, calls=%fused_computation.20.clone.1 | convolution fusion | flops 633779904 | bytes 41048320 | tf_op jit(solution)/shard_map/while/body/eval_jaxpr/cqhd,ckhd->chqk/dot_general | solution.py:188
  801.4 13.7 %multiply_convert_fusion.3 = bf16[4,1104,1104]{1,2,0:T(8,128)(2,1)S(1)} fusion(f32[4,1104,1104]{1,2,0:T(8,128)} %fusion.140, f32[4,1104,1104]{1,2,0:T(8,128)} %get-tuple-element.308, f32[4,1104]{1,0:T(4,128)S(1)} %get-tuple-element.309), kind=kLoop, calls=%fused_computation.19.clone.1 | loop fusion | flops 14625792 | bytes 48770304 | tf_op jit(solution)/shard_map/while/body/eval_jaxpr/convert_element_type | solution.py:192
  823.3 15.4 %convolution_convert_fusion.2 = bf16[1024,3072]{1,0:T(8,128)(2,1)} fusion(bf16[1,1,1104,1024]{3,2,1,0:T(8,128)(2,1)} %param.19, f32[1024]{0:T(1024)S(1)} %bitcast.257, f32[1024]{0:T(1024)S(1)} %bitcast.246, f32[1104]{0:T(1024)S(1)} %copy-done.22, f32[1104]{0:T(1024)S(1)} %copy-done.20, bf16[1104,1024]{0,1:T(8,128)(2,1)} %bitcast.234, ...), kind=kOutput, calls=%fused_computation.75 | convolution fusion | flops 6976045056 | bytes 15352448 | tf_op jit(solution)/shard_map/dot_general | solution.py:27
  838.9 23.1 %reduce-scatter.11.cloned.1.call-done = bf16[1024,1024]{1,0:T(8,128)(2,1)} async-done(((bf16[4096,1024]{1,0:T(8,128)(2,1)}), bf16[1024,1024]{1,0:T(8,128)(2,1)}) %reduce-scatter.11.cloned.1.call-update) | async-done | bytes 2097168 | tf_op jit(solution)/shard_map/reduce_scatter | solution.py:251
  862.1 113.8 %reduce-scatter.5.cloned.1.call-done = bf16[256,3072]{1,0:T(8,128)(2,1)} async-done(((bf16[1024,3072]{1,0:T(8,128)(2,1)}), bf16[256,3072]{1,0:T(8,128)(2,1)}) %reduce-scatter.5.cloned.1.call-update) | async-done | bytes 1572880 | tf_op jit(solution)/shard_map/reduce_scatter | solution.py:227
  1013.3 16.3 %all-reduce.10 = (bf16[1024]{0:T(1024)(128)(2,1)S(1)}, bf16[1024]{0:T(1024)(128)(2,1)S(1)}, bf16[2048]{0:T(1024)(128)(2,1)S(1)}, bf16[1024]{0:T(1024)(128)(2,1)S...) all-reduce(bf16[1024]{0:T(1024)(128)(2,1)S(1)} %get-tuple-element.1, ...), channel_id=3, replica_groups=mesh['rep'=8,'shard'=4] {'shard'}, use_global_device_ids=true, to_apply=%region_16.17.clone | all-reduce | flops 12288 | bytes 49152
  1054.4 16.4 %fusion.72 = bf16[1,1,1104,1024]{3,2,1,0:T(8,128)(2,1)} fusion(f32[1104,1024]{1,0:T(8,128)} %copy-done.7, bf16[1104,4096]{1,0:T(8,128)(2,1)} %get-tuple-element.191, bf16[4096,1024]{1,0:T(8,128)(2,1)} %all-gather.20.cloned.1.call-done, f32[1024]{0:T(1024)S(1)} %bitcast.260, f32[]{:T(128)} %bitcast.22), kind=kOutput, calls=%fused_computation.111 | convolution fusion | flops 9265545216 | bytes 24219652 | tf_op jit(solution)/shard_map/dot_general | solution.py:23
  1079.7 62.6 %all-gather.22.cloned.1.call-done = bf16[2048,3072]{1,0:T(8,128)(2,1)} async-done(((bf16[256,3072]{1,0:T(8,128)(2,1)}), bf16[2048,3072]{1,0:T(8,128)(2,1)}) %all-gather.22.cloned.1.call-update) | async-done | bytes 12582928 | tf_op jit(solution)/shard_map/all_gather | solution.py:57
  (283 shorter events, 479.4 us)
Async XLA Ops:
  7.2 72.2 %copy-start.39 = (bf16[1024]{0:T(1024)(128)(2,1)S(1)}, bf16[1024]{0:T(1024)(128)(2,1)}, u32[]{:S(2)}) copy-start(bf16[1024]{0:T(1024)(128)(2,1)} %param.30) | copy-start | bytes 6148
  7.3 88.8 %copy-start.3 = (bf16[1,1,1104,1024]{3,2,1,0:T(8,128)(2,1)S(1)}, bf16[1,1,1104,1024]{3,2,1,0:T(8,128)(2,1)}, u32[]{:S(2)}) copy-start(bf16[1,1,1104,1024]{3,2,1,0:T(8,128)(2,1)} %param.19) | copy-start | bytes 6782980
  7.3 120.9 %all-gather.14.cloned.1.call-start = ((), (), s32[]{:S(2)}) async-start(), calls=%async_computation.4 | async-start | bytes 7864320 | tf_op jit(solution)/shard_map/all_gather | solution.py:63
  8.0 280.0 %all-gather.16.cloned.1.call-start = ((), (), s32[]{:S(2)}) async-start(), calls=%async_computation.5 | async-start | bytes 2621440 | tf_op jit(solution)/shard_map/all_gather | solution.py:65
  8.7 315.1 %all-gather.18.cloned.1.call-start = ((), (), s32[]{:S(2)}) async-start(), calls=%async_computation.6 | async-start | bytes 10485760 | tf_op jit(solution)/shard_map/all_gather | solution.py:69
  9.5 463.7 %all-gather.20.cloned.1.call-start = ((), (), s32[]{:S(2)}) async-start(), calls=%async_computation.7 | async-start | bytes 10485760 | tf_op jit(solution)/shard_map/all_gather | solution.py:71
  10.1 828.8 %reduce-scatter.7.cloned.1.call-start = ((), (), s32[]{:S(2)}) async-start(), calls=%async_computation.9 | async-start | bytes 2621440 | tf_op jit(solution)/shard_map/reduce_scatter | solution.py:233
  53.3 84.6 %copy-start.35 = (f32[4,1,256]{2,1,0:T(1,128)}, f32[4,1,256]{2,1,0:T(1,128)S(1)}, u32[]{:S(2)}) copy-start(f32[4,1,256]{2,1,0:T(1,128)S(1)} %convert_element_type.232) | copy-start | bytes 12292
  67.3 70.5 %copy-start.29 = (f32[4,1,256]{2,1,0:T(1,128)}, f32[4,1,256]{2,1,0:T(1,128)S(1)}, u32[]{:S(2)}) copy-start(f32[4,1,256]{2,1,0:T(1,128)S(1)} %convert_element_type.231) | copy-start | bytes 12292
  96.4 41.4 %copy-start.19 = (f32[1104]{0:T(1024)}, f32[1104]{0:T(1024)S(1)}, u32[]{:S(2)}) copy-start(f32[1104]{0:T(1024)S(1)} %broadcast_multiply_fusion.1) | copy-start | bytes 13252
  97.8 40.1 %copy-start.21 = (f32[1104]{0:T(1024)}, f32[1104]{0:T(1024)S(1)}, u32[]{:S(2)}) copy-start(f32[1104]{0:T(1024)S(1)} %fusion.75) | copy-start | bytes 13252
  156.2 131.8 %copy-start.38 = (f32[4,1,256]{2,1,0:T(1,128)S(1)}, f32[4,1,256]{2,1,0:T(1,128)}, u32[]{:S(2)}) copy-start(f32[4,1,256]{2,1,0:T(1,128)} %convert_element_type.234) | copy-start | bytes 12292
  323.9 149.3 %copy-start.6 = (bf16[1,1,1104,1024]{3,2,1,0:T(8,128)(2,1)S(1)}, bf16[1,1,1104,1024]{3,2,1,0:T(8,128)(2,1)}, u32[]{:S(2)}) copy-start(bf16[1,1,1104,1024]{3,2,1,0:T(8,128)(2,1)} %param.33) | copy-start | bytes 6782980
  525.9 313.0 %reduce-scatter.9.cloned.1.call-start = ((), (), s32[]{:S(2)}) async-start(), calls=%async_computation.10 | async-start | bytes 10485760 | tf_op jit(solution)/shard_map/reduce_scatter | solution.py:245
  543.9 318.1 %reduce-scatter.11.cloned.1.call-start = ((), (), s32[]{:S(2)}) async-start(), calls=%async_computation.11 | async-start | bytes 10485760 | tf_op jit(solution)/shard_map/reduce_scatter | solution.py:251
  571.8 404.1 %reduce-scatter.5.cloned.1.call-start = ((), (), s32[]{:S(2)}) async-start(), calls=%async_computation.8 | async-start | bytes 7864320 | tf_op jit(solution)/shard_map/reduce_scatter | solution.py:227
  577.1 246.2 %copy-start.20 = (f32[1104]{0:T(1024)S(1)}, f32[1104]{0:T(1024)}, u32[]{:S(2)}) copy-start(f32[1104]{0:T(1024)} %copy-done.19) | copy-start | bytes 13252
  577.1 246.2 %copy-start.22 = (f32[1104]{0:T(1024)S(1)}, f32[1104]{0:T(1024)}, u32[]{:S(2)}) copy-start(f32[1104]{0:T(1024)} %copy-done.21) | copy-start | bytes 13252
  577.1 246.2 %copy-start.30 = (f32[4,1,256]{2,1,0:T(1,128)S(1)}, f32[4,1,256]{2,1,0:T(1,128)}, u32[]{:S(2)}) copy-start(f32[4,1,256]{2,1,0:T(1,128)} %copy-done.29) | copy-start | bytes 12292
  577.1 246.3 %copy-start.36 = (f32[4,1,256]{2,1,0:T(1,128)S(1)}, f32[4,1,256]{2,1,0:T(1,128)}, u32[]{:S(2)}) copy-start(f32[4,1,256]{2,1,0:T(1,128)} %copy-done.35) | copy-start | bytes 12292
  838.8 137.2 %copy-start.49 = (u32[32]{0:T(128)S(1)}, u32[32]{0:T(128)}, u32[]{:S(2)}) copy-start(u32[32]{0:T(128)} %constant.133) | copy-start | bytes 388
  838.8 139.7 %copy-start.48 = (bf16[256]{0:T(256)(128)(2,1)S(1)}, bf16[256]{0:T(256)(128)(2,1)}, u32[]{:S(2)}) copy-start(bf16[256]{0:T(256)(128)(2,1)} %param.32) | copy-start | bytes 1540
  838.8 232.0 %all-reduce.13.cloned.1.call-start = ((), (), s32[]{:S(2)}) async-start(), calls=%async_computation.13 | async-start | bytes 9437184 | tf_op jit(solution)/shard_map/psum | solution.py:264
  862.1 280.2 %all-gather.22.cloned.1.call-start = ((), (), s32[]{:S(2)}) async-start(), calls=%async_computation.12 | async-start | bytes 14155776 | tf_op jit(solution)/shard_map/all_gather | solution.py:57
  (57 other events, 503.2 us)
Sparse Core Ops, SparseCore 0:
  9.7 118.4 all-gather.13
  129.7 44.1 all-gather.15
  175.5 148.3 all-gather.17
  325.3 147.8 all-gather.19
  526.1 42.0 reduce-scatter.6
  570.5 143.7 reduce-scatter.8
  716.8 145.1 reduce-scatter.10
  864.5 111.4 reduce-scatter.4
  980.0 88.2 all-reduce.12
  1070.1 72.1 all-gather.21
